TPU v7x, 256 devices: a whole 4x4x8 slice. The times are simulated.
256 devices in a mesh: seq: 32 (over y, z), tp: 8 (over x, core).
Axes of the slice: x: 4, y: 4, z: 8, core: 2. Of those that a mesh axis runs over, the one named last changes fastest.
Arguments:
- values_in: bfloat16 [16384, 8192], P('seq', 'tp'), may hold values from -6 to 6
- gates_in: bfloat16 [16384, 8192], P('seq', 'tp'), may hold values from -6 to 6
- keys_in: bfloat16 [16384, 1024], P('seq', 'tp'), may hold values from -6 to 6
- queries_in: bfloat16 [16384, 1024], P('seq', 'tp'), may hold values from -6 to 6
- log_decay: float32 [128, 16384], P('tp', 'seq'), may hold values from -2 to 0, as said below
- conv_values: float32 [4, 8192], P(None, 'tp'), may hold values from -3 to 3
- bias_values: float32 [8192], P('tp'), may hold values from -3 to 3
- conv_keys: float32 [4, 1024], P(None, 'tp'), may hold values from -3 to 3
- bias_keys: float32 [1024], P('tp'), may hold values from -3 to 3
- conv_queries: float32 [4, 1024], P(None, 'tp'), may hold values from -3 to 3
- bias_queries: float32 [1024], P('tp'), may hold values from -3 to 3
- skip_scale: float32 [128], P('tp'), may hold values from 0.5 to 1.5
- norm_gain: float32 [8192], P('tp'), may hold values from 0.1 to 1.9
- out_weight: bfloat16 [8192, 4096], P('tp'), may hold values from -0.09375 to 0.09375
Outputs:
- mixer_out: bfloat16 [16384, 4096], P('seq', 'tp')
Inputs may be any that keep to these rules, and one draw needn't show every extreme that they name: `log_decay`: every entry is below zero.
All inputs are finite; a program needn't handle non-finite values.
Results may differ from a plain program's by a relative error of at most 0.015.
Values may be sent and summed in bfloat16 or wider, within the bound.
A program may use at most 64 MiB of HBM per device.

v0:
```python
from functools import partial
import jax
import jax.numpy as jnp
from jax import lax
from jax.sharding import PartitionSpec as P

N = 128
HIGH = lax.Precision.HIGHEST
norm_epsilon = 1e-05


def passed_along(block, axis, distance):
    devices = range(lax.axis_size(axis))
    route = [(i - distance, i) for i in devices if i - distance in devices]
    return lax.ppermute(block, axis, route)


def causal_filter(padded, kernel_weights, conv_bias, row_total):
    width = kernel_weights.shape[0]
    running = jnp.broadcast_to(conv_bias[None, :], (row_total, conv_bias.shape[0]))
    for offset in range(width):
        running = running + kernel_weights[offset][None, :] * padded[
            offset : offset + row_total
        ].astype(jnp.float32)
    return jax.nn.silu(running).astype(jnp.bfloat16)


def block_terms(carried, inputs, per_group):
    values, keys_block, queries, logs = inputs
    row_total = values.shape[0]
    groups = keys_block.shape[1]
    cumulative = jnp.cumsum(logs, axis=1)
    scores = jnp.einsum("tgn,sgn->gts", queries, keys_block, preferred_element_type=jnp.float32)
    positions = lax.broadcasted_iota(jnp.int32, (row_total, row_total), 0)
    sources = lax.broadcasted_iota(jnp.int32, (row_total, row_total), 1)
    log_gaps = jnp.where(
        (positions >= sources)[None], cumulative[:, :, None] - cumulative[:, None, :], -jnp.inf
    )
    mixing = (
        jnp.exp(log_gaps).reshape(groups, per_group, row_total, row_total) * scores[:, None]
    ).astype(jnp.bfloat16)
    local_part = jnp.einsum("ghts,sghp->tghp", mixing, values, preferred_element_type=jnp.float32)
    growth = jnp.exp(cumulative).T.reshape(row_total, groups, per_group, 1)
    from_state = (
        jnp.einsum("tgn,ghnp->tghp", queries.astype(jnp.float32), carried, precision=HIGH) * growth
    )
    remaining = jnp.exp(cumulative[:, -1:] - cumulative).T.reshape(row_total, groups, per_group, 1)
    weighted_keys = keys_block.astype(jnp.float32)[:, :, None, :] * remaining
    fresh_state = jnp.einsum(
        "tghn,tghp->ghnp", weighted_keys, values.astype(jnp.float32), precision=HIGH
    )
    carried = jnp.exp(cumulative[:, -1]).reshape(groups, per_group, 1, 1) * carried + fresh_state
    return (carried, local_part + from_state)


def shards(
    values_in,
    gates_in,
    keys_in,
    queries_in,
    log_decay,
    conv_values,
    bias_values,
    conv_keys,
    bias_keys,
    conv_queries,
    bias_queries,
    skip_scale,
    norm_gain,
    out_weight,
):
    row_total = values_in.shape[0]
    head_count = log_decay.shape[0]
    inner_width = values_in.shape[1]
    head_size = inner_width // head_count
    key_width = keys_in.shape[1]
    groups = key_width // N
    per_group = head_count // groups
    margin = conv_values.shape[0] - 1
    rim_send = jnp.concatenate(
        [
            values_in[row_total - margin :],
            keys_in[row_total - margin :],
            queries_in[row_total - margin :],
        ],
        axis=1,
    )
    rim_rows = passed_along(rim_send, "seq", 1)
    values = causal_filter(
        jnp.concatenate([rim_rows[:, :inner_width], values_in], axis=0),
        conv_values,
        bias_values,
        row_total,
    )
    keys_all = causal_filter(
        jnp.concatenate([rim_rows[:, inner_width : inner_width + key_width], keys_in], axis=0),
        conv_keys,
        bias_keys,
        row_total,
    )
    queries_all = causal_filter(
        jnp.concatenate([rim_rows[:, inner_width + key_width :], queries_in], axis=0),
        conv_queries,
        bias_queries,
        row_total,
    )
    block_rows = min(row_total, 512)
    block_count = row_total // block_rows
    value_blocks = values.reshape(block_count, block_rows, groups, per_group, head_size)
    key_blocks = keys_all.reshape(block_count, block_rows, groups, N)
    query_blocks = queries_all.reshape(block_count, block_rows, groups, N)
    log_blocks = log_decay.reshape(head_count, block_count, block_rows).transpose(1, 0, 2)
    initial = jnp.zeros((groups, per_group, N, head_size), jnp.float32)
    local_end, outputs = lax.scan(
        partial(block_terms, per_group=per_group),
        initial,
        (value_blocks, key_blocks, query_blocks, log_blocks),
    )
    cumulative = jnp.cumsum(log_decay, axis=1)
    device_log = cumulative[:, -1]
    flat_end = local_end.reshape(head_count, N * head_size)
    all_logs = lax.all_gather(device_log[None, :], "seq", axis=0, tiled=True)
    inclusive = jnp.cumsum(all_logs, axis=0)
    own_index = lax.axis_index("seq")
    before_mine = lax.dynamic_index_in_dim(inclusive - all_logs, own_index, 0, keepdims=False)
    pieces = lax.all_gather(flat_end[None].astype(jnp.bfloat16), "seq", axis=0, tiled=True).astype(
        jnp.float32
    )
    shard_ids = jnp.arange(pieces.shape[0], dtype=jnp.int32)
    through_shard = jnp.take(inclusive, shard_ids, axis=0)
    exponent = jnp.where(
        (shard_ids < own_index)[:, None], before_mine[None, :] - through_shard, -jnp.inf
    )
    incoming = jnp.zeros_like(flat_end) + jnp.einsum(
        "kh,khm->hm", jnp.exp(exponent), pieces, precision=HIGH
    )
    incoming = incoming.reshape(groups, per_group, N, head_size)
    growth = jnp.exp(cumulative).T.reshape(row_total, groups, per_group, 1)
    query_rows = queries_all.reshape(row_total, groups, N).astype(jnp.float32)
    from_before = jnp.einsum("tgn,ghnp->tghp", query_rows, incoming, precision=HIGH) * growth
    mixed = outputs.reshape(row_total, groups, per_group, head_size) + from_before
    mixed = mixed + skip_scale.reshape(groups, per_group)[None, :, :, None] * values.reshape(
        row_total, groups, per_group, head_size
    ).astype(jnp.float32)
    gated_rows = mixed.reshape(row_total, groups, per_group * head_size) * jax.nn.silu(
        gates_in.reshape(row_total, groups, per_group * head_size).astype(jnp.float32)
    )
    mean_square = jnp.mean(gated_rows * gated_rows, axis=-1, keepdims=True)
    normed = (
        (
            gated_rows
            * lax.rsqrt(mean_square + norm_epsilon)
            * norm_gain.reshape(groups, per_group * head_size)
        )
        .astype(jnp.bfloat16)
        .reshape(row_total, inner_width)
    )
    local_sum = jnp.dot(normed, out_weight, preferred_element_type=jnp.float32)
    summed = lax.psum(local_sum.astype(jnp.bfloat16), "tp").astype(jnp.float32)
    column_width = summed.shape[1] // lax.axis_size("tp")
    result = lax.dynamic_slice_in_dim(summed, lax.axis_index("tp") * column_width, column_width, 1)
    return result.astype(jnp.bfloat16)


def solution(mesh):
    placed = (
        P("seq", "tp"),
        P("seq", "tp"),
        P("seq", "tp"),
        P("seq", "tp"),
        P("tp", "seq"),
        P(None, "tp"),
        P("tp"),
        P(None, "tp"),
        P("tp"),
        P(None, "tp"),
        P("tp"),
        P("tp"),
        P("tp"),
        P("tp", None),
    )
    return jax.shard_map(
        shards, mesh=mesh, in_specs=placed, out_specs=P("seq", "tp"), check_vma=False
    )
```

profile of v0, /device:TPU:8, one launch (start us, length us, event | category | flops | bytes accessed | tf_op | source)
XLA Modules:
  0.0 248.3 jit_solution(196115072066289706)
XLA Ops:
  6.6 0.8 slice.96
  7.4 0.7 slice.97
  8.1 0.7 slice.98
  8.8 0.3 copy.48
  9.0 3.8 %collective-permute-start = (bf16[3,1280]{0,1:T(8,128)(2,1)S(1)}, bf16[3,1280]{0,1:T(8,128)(2,1)S(1)}, u32[]{:S(2)}, u32[]{:S(2)}) collective-permute-start(bf16[3,1280]{0,1:T(8,128)(2,1)S(1)} %copy.48), channel_id=1, source_target_pairs={{0,8},{8,16},{16,24},{24,32},{32,40},{40,48},{48,56},{56,64},{64,7... | collective-permute-start | bytes 23048 | tf_op jit(solution)/shard_map/ppermute | solution.py:15
  12.9 1.2 reduce-window.12
  14.5 0.9 fusion.41
  15.4 0.8 slice_bitcast_fusion.3
  16.3 1.5 copy.49
  17.8 6.5 %collective-permute-done = bf16[3,1280]{0,1:T(8,128)(2,1)S(1)} collective-permute-done((bf16[3,1280]{0,1:T(8,128)(2,1)S(1)}, bf16[3,1280]{0,1:T(8,128)(2,1)S(1)}, u32[]{:S(2)}, u32[]{:S(2)}) %collective-permute-start) | collective-permute-done | bytes 7712 | tf_op jit(solution)/shard_map/ppermute | solution.py:15
  24.7 2.7 %multiply_convert_fusion.3 = bf16[512,1024]{0,1:T(8,128)(2,1)S(1)} fusion(bf16[512,1024]{0,1:T(8,128)(2,1)S(1)} %copy.49, bf16[3,1024]{0,1:T(8,128)(2,1)S(1)} %slice.127, f32[1024]{0:T(1024)S(1)} %bitcast.91, f32[1024]{0:T(1024)S(1)} %bitcast.92, f32[1024]{0:T(1024)S(1)} %bitcast.90, f32[1024]{0:T(1024)S(1)} %bitcast.89, f32[1024]{0:T(1024)S(1)} %copy-done.7), kind=kLoop, calls=%fused_computation.25 | loop fusion | flops 13631488 | bytes 2123776 | tf_op jit(solution)/shard_map/convert_element_type | solution.py:25
  27.4 2.4 fusion.18
  29.9 0.3 copy.55
  30.1 1.2 convert_element_type.126
  31.4 0.6 dynamic-slice.1
  32.9 62.4 %all-reduce = f32[512]{0:T(512)S(1)} all-reduce(f32[512]{0:T(512)S(1)} %dynamic-update-slice), channel_id=2, replica_groups=mesh['seq'=32,'tp'=8] {'seq'}, use_global_device_ids=true, to_apply=%add | all-reduce | flops 512 | bytes 4096
  95.5 0.6 gather_fusion
  96.3 1.3 copy.57
  97.6 0.8 iota_compare_fusion
  98.7 0.3 fusion.42
  99.0 1.0 fusion.25
  100.0 5.8 %fusion.2 = f32[16,64,512]{2,1,0:T(8,128)} fusion(bf16[512,16,64]{0,2,1:T(8,128)(2,1)S(1)} %bitcast.86, f32[512,512]{1,0:T(8,128)S(1)} %fusion.42, f32[16,512]{1,0:T(8,128)S(1)} %copy_bitcast_fusion.1, pred[512,512]{1,0:T(8,128)(4,1)S(1)} %copy-done.4), kind=kOutput, calls=%fused_computation.4 | convolution fusion | flops 553648128 | bytes 4489216 | tf_op jit(solution)/shard_map/while/body/eval_jaxpr/ghts,sghp->tghp/dot_general | solution.py:42
  105.8 22.5 %all-gather.3.cloned.1.call-done = bf16[32,16,8192]{2,1,0:T(8,128)(2,1)} async-done(((bf16[1,16,8192]{2,1,0:T(8,128)(2,1)}), bf16[32,16,8192]{2,1,0:T(8,128)(2,1)}) %all-gather.3.cloned.1.call-update) | async-done | bytes 8388624 | tf_op jit(solution)/shard_map/all_gather | solution.py:126
  128.3 16.9 %fusion = f32[16,1,8192]{2,1,0:T(1,128)S(1)} fusion(f32[32,16,1]{0,2,1:T(1,128)S(1)} %copy.58, bf16[32,16,8192]{2,1,0:T(8,128)(2,1)} %all-gather.3.cloned.1.call-done), kind=kOutput, calls=%fused_computation.2 | convolution fusion | flops 50331648 | bytes 8914944 | tf_op jit(solution)/shard_map/kh,khm->hm/dot_general | solution.py:134
  145.2 1.1 copy.73
  146.3 2.5 reshape.210
  148.7 3.2 %fusion.31 = f32[16,64,512]{2,1,0:T(8,128)S(1)} fusion(f32[16,128,64]{2,1,0:T(8,128)} %reshape.210, bf16[512,128]{1,0:T(8,128)(2,1)S(1)} %multiply_convert_fusion.6), kind=kOutput, calls=%fused_computation.54 | convolution fusion | flops 805306368 | bytes 2752512 | tf_op jit(solution)/shard_map/tgn,ghnp->tghp/dot_general | solution.py:140
  152.0 1.0 fusion.10
  153.2 0.7 multiply_reduce_fusion
  153.9 9.7 %convolution_convert_fusion = bf16[512,4096]{1,0:T(8,128)(2,1)} fusion(bf16[1024,4096]{1,0:T(8,128)(2,1)} %param.27, f32[512,1024]{0,1:T(8,128)S(1)} %get-tuple-element.18, f32[1024]{0:T(1024)S(1)} %copy-done.12, f32[512]{0:T(512)S(1)} %add_rsqrt_fusion), kind=kOutput, calls=%fused_computation.6 | convolution fusion | flops 4298637312 | bytes 14686208 | tf_op jit(solution)/shard_map/dot_general | solution.py:158
  163.7 75.9 %all-reduce.3.cloned.1.call-done = bf16[512,4096]{1,0:T(8,128)(2,1)} async-done(((bf16[512,4096]{1,0:T(8,128)(2,1)}), bf16[512,4096]{1,0:T(8,128)(2,1)}) %all-reduce.3.cloned.1.call-update) | async-done | bytes 4194320 | tf_op jit(solution)/shard_map/psum | solution.py:159
  239.6 1.9 convert_convert_fusion
  (59 shorter events, 2.1 us)
Async XLA Ops:
  6.5 6.3 %copy-start = (f32[16,512]{1,0:T(8,128)S(1)}, f32[16,512]{1,0:T(8,128)}, u32[]{:S(2)}) copy-start(f32[16,512]{1,0:T(8,128)} %param.18) | copy-start | bytes 98308
  6.5 17.9 %copy-start.5 = (bf16[512,128]{1,0:T(8,128)(2,1)S(1)}, bf16[512,128]{1,0:T(8,128)(2,1)}, u32[]{:S(2)}) copy-start(bf16[512,128]{1,0:T(8,128)(2,1)} %param.16) | copy-start | bytes 393220
  6.5 17.9 %copy-start.9 = (f32[128]{0:T(128)S(1)}, f32[128]{0:T(128)}, u32[]{:S(2)}) copy-start(f32[128]{0:T(128)} %param.22) | copy-start | bytes 1540
  6.5 18.2 %copy-start.7 = (f32[1024]{0:T(1024)S(1)}, f32[1024]{0:T(1024)}, u32[]{:S(2)}) copy-start(f32[1024]{0:T(1024)} %param.20) | copy-start | bytes 12292
  6.5 121.8 %all-gather.3.cloned.1.call-start = ((), (), s32[]{:S(2)}) async-start(), calls=%async_computation | async-start | bytes 8650752 | tf_op jit(solution)/shard_map/all_gather | solution.py:126
  9.0 15.4 %collective-permute-start = (bf16[3,1280]{0,1:T(8,128)(2,1)S(1)}, bf16[3,1280]{0,1:T(8,128)(2,1)S(1)}, u32[]{:S(2)}, u32[]{:S(2)}) collective-permute-start(bf16[3,1280]{0,1:T(8,128)(2,1)S(1)} %copy.48), channel_id=1, source_target_pairs={{0,8},{8,16},{16,24},{24,32},{32,40},{40,48},{48,56},{56,64},{64,7... | collective-permute-start | bytes 23048 | tf_op jit(solution)/shard_map/ppermute | solution.py:15
  27.4 4.0 %copy-start.13 = (u32[256]{0:T(256)S(1)}, u32[256]{0:T(256)}, u32[]{:S(2)}) copy-start(u32[256]{0:T(256)} %constant.80) | copy-start | bytes 3076
  27.4 68.9 %copy-start.3 = (bf16[512,1024]{1,0:T(8,128)(2,1)S(1)}, bf16[512,1024]{1,0:T(8,128)(2,1)}, u32[]{:S(2)}) copy-start(bf16[512,1024]{1,0:T(8,128)(2,1)} %param.15) | copy-start | bytes 3145732
  29.8 68.6 %copy-start.8 = (f32[4,128]{1,0:T(4,128)S(1)}, f32[4,128]{1,0:T(4,128)}, u32[]{:S(2)}) copy-start(f32[4,128]{1,0:T(4,128)} %param.23) | copy-start | bytes 6148
  29.8 68.7 %copy-start.6 = (bf16[512,128]{1,0:T(8,128)(2,1)S(1)}, bf16[512,128]{1,0:T(8,128)(2,1)}, u32[]{:S(2)}) copy-start(bf16[512,128]{1,0:T(8,128)(2,1)} %param.17) | copy-start | bytes 393220
  29.8 68.7 %copy-start.10 = (f32[128]{0:T(128)S(1)}, f32[128]{0:T(128)}, u32[]{:S(2)}) copy-start(f32[128]{0:T(128)} %param.24) | copy-start | bytes 1540
  31.4 208.2 %all-reduce.3.cloned.1.call-start = ((), (), s32[]{:S(2)}) async-start(), calls=%async_computation.1 | async-start | bytes 8388608 | tf_op jit(solution)/shard_map/psum | solution.py:159
  98.5 1.5 copy-start.4
  146.3 5.7 %copy-start.11 = (f32[16]{0:T(128)S(1)}, f32[16]{0:T(128)}, u32[]{:S(2)}) copy-start(f32[16]{0:T(128)} %param.25) | copy-start | bytes 196
  148.7 3.2 %copy-start.2 = (f32[16,64,512]{2,1,0:T(8,128)S(1)}, f32[16,64,512]{2,1,0:T(8,128)}, u32[]{:S(2)}) copy-start(f32[16,64,512]{2,1,0:T(8,128)} %fusion.2) | copy-start | bytes 6291460
  152.0 1.2 copy-start.1
  153.2 0.7 copy-start.12
Sparse Core Ops, SparseCore 0:
  31.5 96.7 all-gather.2
  163.8 75.7 all-reduce.2
where the time goes:
time: 249 us; the launch traced here: 248 us
  waiting for transfers between devices  105 us (42%)
  blocking collectives  62.4 us (25%)
  matrix products  39.3 us (16%)
  local copies, waits for them, and re-layouts  14.4 us (6%)
  between operations  14.3 us (6%)
  other arithmetic  8.96 us (4%)
  starting transfers between devices  3.9 us (2%)
    psum x1, waiting for transfers between devices, shards(): summed = lax.psum(local_sum.astype(jnp.bfloat16), 'tp').astype(jnp.float32)  75.9 us
    unnamed x1, blocking collectives  62.4 us
    all_gather x1, waiting for transfers between devices, shards(): lax.all_gather(flat_end[None].astype(jnp.bfloat16), 'seq', axis=0, tiled=...  22.5 us
    dot_general x1, matrix products, shards(): jnp.einsum('kh,khm->hm', jnp.exp(exponent), pieces, precision=HIGH)  16.9 us
    dot_general x1, matrix products, shards(): local_sum = jnp.dot(normed, out_weight, preferred_element_type=jnp.float32)  9.74 us
    ppermute x1, waiting for transfers between devices, passed_along(): return lax.ppermute(block, axis, route)  6.53 us
    dot_general x1, matrix products, block_terms(): jnp.einsum('ghts,sghp->tghp', mixing, values, preferred_element_type=jnp....  5.8 us
  transfers between devices with their start and end apart: 3, of which 3 were waited for; matrix products, arithmetic and copies ran while one was open for 7% of the time, Pallas kernels for 0%

commit v1 on v0

--- a/solution.py
+++ b/solution.py
@@ -7,6 +7,14 @@
 N = 128
 HIGH = lax.Precision.HIGHEST
 norm_epsilon = 1e-05
+
+
+def gather_from_all(array, axis, dim):
+    size = lax.axis_size(axis)
+    repeats = [size if d == dim else 1 for d in range(array.ndim)]
+    return lax.all_to_all(
+        jnp.tile(array, repeats), axis, split_axis=dim, concat_axis=dim, tiled=True
+    )
 
 
 def passed_along(block, axis, distance):
@@ -123,9 +131,7 @@
     inclusive = jnp.cumsum(all_logs, axis=0)
     own_index = lax.axis_index("seq")
     before_mine = lax.dynamic_index_in_dim(inclusive - all_logs, own_index, 0, keepdims=False)
-    pieces = lax.all_gather(flat_end[None].astype(jnp.bfloat16), "seq", axis=0, tiled=True).astype(
-        jnp.float32
-    )
+    pieces = gather_from_all(flat_end[None].astype(jnp.bfloat16), "seq", 0).astype(jnp.float32)
     shard_ids = jnp.arange(pieces.shape[0], dtype=jnp.int32)
     through_shard = jnp.take(inclusive, shard_ids, axis=0)
     exponent = jnp.where(

time: 249 us -> 420 us (1.69)
  blocking collectives: 62.4 us -> 239 us
  waiting for transfers between devices: 105 us -> 87.4 us
  starting transfers between devices: 3.9 us -> 13 us
    unnamed x1, blocking collectives: 62.4 us -> 239 us
    all_gather x1 -> x0, waiting for transfers between devices: 22.5 us -> none  [shards(): lax.all_gather(flat_end[None].astype(jnp.bfloat16), 'seq', axis=0, tiled=...]
    all_to_all x0 -> x1, starting transfers between devices: none -> 9.09 us  [gather_from_all(): lax.all_to_all(jnp.tile(array, repeats), axis, split_axis=dim, concat_axi...]
    psum x1, waiting for transfers between devices: 75.9 us -> 80.9 us  [shards(): summed = lax.psum(local_sum.astype(jnp.bfloat16), 'tp').astype(jnp.float32)]
    another operation x4 -> x5, local copies, waits for them, and re-layouts: 2.61 us -> 6.84 us  [the longest x1 4.24 us: gather_from_all(): jnp.tile(array, repeats)]
  transfers between devices with their start and end apart: 3 -> 3, of which waited for: 3 -> 2; matrix products, arithmetic and copies ran while one was open for 7% -> 4% of each run, Pallas kernels for 0% -> 0%
where the time goes in v1:
time: 420 us; the launch traced here: 419 us
  blocking collectives  239 us (57%)
  waiting for transfers between devices  87.4 us (21%)
  matrix products  39.3 us (9%)
  local copies, waits for them, and re-layouts  17.9 us (4%)
  between operations  14.4 us (3%)
  starting transfers between devices  13 us (3%)
  other arithmetic  8.93 us (2%)
    unnamed x1, blocking collectives  239 us
    psum x1, waiting for transfers between devices, shards(): summed = lax.psum(local_sum.astype(jnp.bfloat16), 'tp').astype(jnp.float32)  80.9 us
    dot_general x1, matrix products, shards(): jnp.einsum('kh,khm->hm', jnp.exp(exponent), pieces, precision=HIGH)  16.9 us
    dot_general x1, matrix products, shards(): local_sum = jnp.dot(normed, out_weight, preferred_element_type=jnp.float32)  9.73 us
    all_to_all x1, starting transfers between devices, gather_from_all(): lax.all_to_all(jnp.tile(array, repeats), axis, split_axis=dim, concat_axi...  9.09 us
  transfers between devices with their start and end apart: 3, of which 2 were waited for; matrix products, arithmetic and copies ran while one was open for 4% of the time, Pallas kernels for 0%

profile of v1, /device:TPU:8, one launch (start us, length us, event | category | flops | bytes accessed | tf_op | source)
XLA Modules:
  0.0 419.5 jit_solution(12147121156892636644)
XLA Ops:
  6.5 0.8 slice.96
  7.3 0.7 slice.97
  8.0 0.7 slice.98
  8.9 3.8 collective-permute-start
  12.8 1.2 reduce-window.12
  14.4 0.9 fusion.41
  15.3 0.8 slice_bitcast_fusion.3
  16.3 1.5 copy.49
  17.8 6.5 %collective-permute-done = bf16[3,1280]{0,1:T(8,128)(2,1)S(1)} collective-permute-done((bf16[3,1280]{0,1:T(8,128)(2,1)S(1)}, bf16[3,1280]{0,1:T(8,128)(2,1)S(1)}, u32[]{:S(2)}, u32[]{:S(2)}) %collective-permute-start) | collective-permute-done | bytes 7712 | tf_op jit(solution)/shard_map/ppermute | solution.py:23
  24.6 2.7 multiply_convert_fusion.3
  27.3 2.4 fusion.18
  29.7 0.3 copy.55
  30.0 0.5 convert_element_type.124
  30.5 4.2 %tile.2 = bf16[32,16,8192]{2,1,0:T(8,128)(2,1)} broadcast(bf16[16,8192]{1,0:T(8,128)(2,1)S(1)} %convert_element_type.124), dimensions={1,2} | broadcast | bytes 8650752 | tf_op jit(solution)/shard_map/tile | solution.py:16
  34.7 9.1 %all-to-all-start = ((bf16[32,16,8192]{2,1,0:T(8,128)(2,1)}), bf16[32,16,8192]{2,1,0:T(8,128)(2,1)}, u32[]{:S(2)}, u32[]{:S(2)}) async-start(bf16[32,16,8192]{2,1,0:T(8,128)(2,1)} %tile.2), calls=%async_computation | async-start | bytes 16777216 | tf_op jit(solution)/shard_map/all_to_all | solution.py:15
  43.9 0.6 dynamic-slice.1
  45.4 238.6 %all-reduce = f32[512]{0:T(512)S(1)} all-reduce(f32[512]{0:T(512)S(1)} %dynamic-update-slice), channel_id=2, replica_groups=mesh['seq'=32,'tp'=8] {'seq'}, use_global_device_ids=true, to_apply=%add | all-reduce | flops 512 | bytes 4096
  284.2 0.6 gather_fusion
  285.0 1.3 copy.57
  286.3 0.8 iota_compare_fusion
  287.4 0.3 fusion.42
  287.7 1.0 fusion.25
  288.7 5.8 %fusion.2 = f32[16,64,512]{2,1,0:T(8,128)} fusion(bf16[512,16,64]{0,2,1:T(8,128)(2,1)S(1)} %bitcast.86, f32[512,512]{1,0:T(8,128)S(1)} %fusion.42, f32[16,512]{1,0:T(8,128)S(1)} %copy_bitcast_fusion.1, pred[512,512]{1,0:T(8,128)(4,1)S(1)} %copy-done.4), kind=kOutput, calls=%fused_computation.4 | convolution fusion | flops 553648128 | bytes 4489216 | tf_op jit(solution)/shard_map/while/body/eval_jaxpr/ghts,sghp->tghp/dot_general | solution.py:50
  294.5 16.9 %fusion = f32[16,1,8192]{2,1,0:T(1,128)S(1)} fusion(f32[32,16,1]{0,2,1:T(1,128)S(1)} %copy.58, bf16[32,16,8192]{2,1,0:T(8,128)(2,1)} %all-to-all-done), kind=kOutput, calls=%fused_computation.2 | convolution fusion | flops 50331648 | bytes 8914944 | tf_op jit(solution)/shard_map/kh,khm->hm/dot_general | solution.py:140
  311.4 1.1 copy.73
  312.5 2.4 reshape.208
  314.9 3.2 fusion.31
  318.2 1.0 fusion.10
  319.4 0.7 multiply_reduce_fusion
  320.1 9.7 %convolution_convert_fusion = bf16[512,4096]{1,0:T(8,128)(2,1)} fusion(bf16[1024,4096]{1,0:T(8,128)(2,1)} %param.27, f32[512,1024]{0,1:T(8,128)S(1)} %get-tuple-element.18, f32[1024]{0:T(1024)S(1)} %copy-done.12, f32[512]{0:T(512)S(1)} %add_rsqrt_fusion), kind=kOutput, calls=%fused_computation.6 | convolution fusion | flops 4298637312 | bytes 14686208 | tf_op jit(solution)/shard_map/dot_general | solution.py:164
  329.9 80.9 %all-reduce.3.cloned.1.call-done = bf16[512,4096]{1,0:T(8,128)(2,1)} async-done(((bf16[512,4096]{1,0:T(8,128)(2,1)}), bf16[512,4096]{1,0:T(8,128)(2,1)}) %all-reduce.3.cloned.1.call-update) | async-done | bytes 4194320 | tf_op jit(solution)/shard_map/psum | solution.py:165
  410.7 1.9 convert_convert_fusion
  (59 shorter events, 2.3 us)
Async XLA Ops:
  6.5 6.3 %copy-start = (f32[16,512]{1,0:T(8,128)S(1)}, f32[16,512]{1,0:T(8,128)}, u32[]{:S(2)}) copy-start(f32[16,512]{1,0:T(8,128)} %param.18) | copy-start | bytes 98308
  6.5 17.8 %copy-start.5 = (bf16[512,128]{1,0:T(8,128)(2,1)S(1)}, bf16[512,128]{1,0:T(8,128)(2,1)}, u32[]{:S(2)}) copy-start(bf16[512,128]{1,0:T(8,128)(2,1)} %param.16) | copy-start | bytes 393220
  6.5 17.9 %copy-start.9 = (f32[128]{0:T(128)S(1)}, f32[128]{0:T(128)}, u32[]{:S(2)}) copy-start(f32[128]{0:T(128)} %param.22) | copy-start | bytes 1540
  6.5 18.1 %copy-start.7 = (f32[1024]{0:T(1024)S(1)}, f32[1024]{0:T(1024)}, u32[]{:S(2)}) copy-start(f32[1024]{0:T(1024)} %param.20) | copy-start | bytes 12292
  8.9 15.4 %collective-permute-start = (bf16[3,1280]{0,1:T(8,128)(2,1)S(1)}, bf16[3,1280]{0,1:T(8,128)(2,1)S(1)}, u32[]{:S(2)}, u32[]{:S(2)}) collective-permute-start(bf16[3,1280]{0,1:T(8,128)(2,1)S(1)} %copy.48), channel_id=1, source_target_pairs={{0,8},{8,16},{16,24},{24,32},{32,40},{40,48},{48,56},{56,64},{64,7... | collective-permute-start | bytes 23048 | tf_op jit(solution)/shard_map/ppermute | solution.py:23
  34.7 9.2 %copy-start.13 = (u32[256]{0:T(256)S(1)}, u32[256]{0:T(256)}, u32[]{:S(2)}) copy-start(u32[256]{0:T(256)} %constant.80) | copy-start | bytes 3076
  34.7 250.2 %copy-start.3 = (bf16[512,1024]{1,0:T(8,128)(2,1)S(1)}, bf16[512,1024]{1,0:T(8,128)(2,1)}, u32[]{:S(2)}) copy-start(bf16[512,1024]{1,0:T(8,128)(2,1)} %param.15) | copy-start | bytes 3145732
  34.7 259.8 %all-to-all-start = ((bf16[32,16,8192]{2,1,0:T(8,128)(2,1)}), bf16[32,16,8192]{2,1,0:T(8,128)(2,1)}, u32[]{:S(2)}, u32[]{:S(2)}) async-start(bf16[32,16,8192]{2,1,0:T(8,128)(2,1)} %tile.2), calls=%async_computation | async-start | bytes 16777216 | tf_op jit(solution)/shard_map/all_to_all | solution.py:15
  43.8 243.3 %copy-start.8 = (f32[4,128]{1,0:T(4,128)S(1)}, f32[4,128]{1,0:T(4,128)}, u32[]{:S(2)}) copy-start(f32[4,128]{1,0:T(4,128)} %param.23) | copy-start | bytes 6148
  43.8 243.3 %copy-start.6 = (bf16[512,128]{1,0:T(8,128)(2,1)S(1)}, bf16[512,128]{1,0:T(8,128)(2,1)}, u32[]{:S(2)}) copy-start(bf16[512,128]{1,0:T(8,128)(2,1)} %param.17) | copy-start | bytes 393220
  43.8 243.3 %copy-start.10 = (f32[128]{0:T(128)S(1)}, f32[128]{0:T(128)}, u32[]{:S(2)}) copy-start(f32[128]{0:T(128)} %param.24) | copy-start | bytes 1540
  43.9 366.9 %all-reduce.3.cloned.1.call-start = ((), (), s32[]{:S(2)}) async-start(), calls=%async_computation.1 | async-start | bytes 8388608 | tf_op jit(solution)/shard_map/psum | solution.py:165
  287.2 1.5 copy-start.4
  312.5 5.7 %copy-start.11 = (f32[16]{0:T(128)S(1)}, f32[16]{0:T(128)}, u32[]{:S(2)}) copy-start(f32[16]{0:T(128)} %param.25) | copy-start | bytes 196
  314.9 3.2 copy-start.2
  318.2 1.2 copy-start.1
  319.4 0.7 copy-start.12
Sparse Core Ops, SparseCore 0:
  330.0 80.7 all-reduce.2
